TPU v7x, 32 devices: a whole 2x2x4 slice. The times are simulated.
32 devices in a mesh: groups: 2 (over x), ctx: 8 (over z, y), head: 2 (over core).
Axes of the slice: x: 2, y: 2, z: 4, core: 2. Of those that a mesh axis runs over, the one named last changes fastest.
Arguments:
- queries: bfloat16 [4096, 2048], P(('groups', 'ctx'), 'head'), parts along dimension 0, may hold values from -12 to 12
- span_keys: bfloat16 [4096, 2048], P(('groups', 'ctx'), 'head'), parts along dimension 0, may hold values from -12 to 12
- span_values: bfloat16 [4096, 2048], P(('groups', 'ctx'), 'head'), parts along dimension 0, may hold values from -6 to 6
- cache_keys: bfloat16 [8192, 2048], P(('groups', 'ctx'), 'head'), parts along dimension 0, may hold values from -12 to 12
- cache_values: bfloat16 [8192, 2048], P(('groups', 'ctx'), 'head'), parts along dimension 0, may hold values from -6 to 6
- routes: int32 [2, 32, 8, 4], P('head', ('groups', 'ctx')), parts along dimension 1, may hold values from 0 to 7, all different within a row; in each aligned block of 16 rows (0 to 15, 16 to 31, ..., all dimensions but the last counted through in order) at most 16 rows name the same one
- out_weight: bfloat16 [2048, 4096], P('head'), may hold values from -0.125 to 0.125
Outputs:
- projected: bfloat16 [4096, 4096], P(('groups', 'ctx'), 'head'), parts along dimension 0
There are 2 independent parts, one for each index of `groups`. A program takes and returns all parts, laid end to end along the dimension named above; an argument that names none is the same for every part. Nothing has to cross between parts.
Inputs may be any that keep to these rules, and one draw needn't show every extreme that they name: `routes`: each row names 4 different key blocks; among the 16 rows of one device no key block is named more than 16 times.
All inputs are finite; a program needn't handle non-finite values.
Results may differ from a plain program's by a relative error of at most 0.0064.
Values may be sent and summed in bfloat16 or wider, within the bound.
A program may use at most 128 MiB of HBM per device.

v0:
```python
import math

import jax
import jax.numpy as jnp
from jax import lax
from jax.sharding import PartitionSpec as P

DH = 128
QB = 128


def shortened(value):

    def short(part):
        return part.astype(jnp.bfloat16) if part.dtype == jnp.float32 else part

    return jax.tree.map(short, value)


def soft_partial(scores, values_block, pattern):
    highest = jnp.max(scores, axis=-1, keepdims=True)
    exponent = jnp.exp(scores - highest)
    denominator = jnp.sum(exponent, axis=-1, keepdims=True)
    weights_low = (exponent / denominator).astype(jnp.bfloat16)
    result = jnp.einsum(
        pattern, weights_low, values_block, preferred_element_type=jnp.float32
    ).astype(jnp.bfloat16)
    log_total = highest[..., 0] + jnp.log(denominator[..., 0])
    return (result, log_total)


def on_device(queries, span_keys, span_values, cache_keys, cache_values, routes, out_weight):
    blocks = routes.shape[1]
    heads_here = routes.shape[2]
    top_picks = routes.shape[3]
    key_rows = cache_keys.shape[0]
    devices = lax.axis_size("ctx")
    scaling = 1.0 / math.sqrt(DH)
    blocked = queries.reshape(blocks, QB, heads_here, DH)
    most_rows = max(2, 2 * blocks * heads_here * top_picks // devices)
    groups = 1
    per_peer = groups * most_rows
    slot_total = per_peer * devices
    wanted = routes.reshape(-1)
    item_count = wanted.shape[0]
    item_ids = jnp.arange(item_count, dtype=jnp.int32)
    block_of = item_ids // (heads_here * top_picks)
    head_of = item_ids // top_picks % heads_here
    bucket = wanted * groups + block_of % groups
    one_hot = (bucket[:, None] == jnp.arange(devices * groups, dtype=jnp.int32)[None, :]).astype(
        jnp.int32
    )
    ranking = jnp.sum(jnp.cumsum(one_hot, axis=0) * one_hot, axis=1) - 1
    position = (block_of % groups * most_rows + ranking) * devices + wanted
    matches = position[None, :] == jnp.arange(slot_total, dtype=jnp.int32)[:, None]
    filled = jnp.any(matches, axis=1)
    source = jnp.sum(jnp.where(matches, item_ids[None, :], 0), axis=1)
    gathered = blocked[block_of[source], :, head_of[source], :]
    slot_queries = jnp.where(filled[:, None, None], gathered, jnp.zeros_like(gathered)).reshape(
        per_peer, devices, QB, DH
    )
    slot_heads = jnp.where(filled, head_of[source], 0).reshape(per_peer, devices)
    keys_by_head = cache_keys.reshape(key_rows, heads_here, DH).transpose(1, 0, 2)
    values_by_head = cache_values.reshape(key_rows, heads_here, DH).transpose(1, 0, 2)

    def one_portion(portion):
        queried, head_ids = portion
        chosen_keys = keys_by_head[head_ids]
        chosen_values = values_by_head[head_ids]
        scores = (
            jnp.einsum("pqd,pkd->pqk", queried, chosen_keys, preferred_element_type=jnp.float32)
            * scaling
        )
        return soft_partial(scores, chosen_values, "pqk,pkd->pqd")

    outputs, log_sums = lax.map(
        one_portion,
        (
            lax.all_to_all(slot_queries, "ctx", split_axis=1, concat_axis=1, tiled=True),
            lax.all_to_all(slot_heads, "ctx", split_axis=1, concat_axis=1, tiled=True),
        ),
    )
    outputs_back = jax.tree.map(
        lambda part, own: part.astype(own.dtype),
        lax.all_to_all(shortened(outputs), "ctx", split_axis=1, concat_axis=1, tiled=True),
        outputs,
    )
    sums_back = lax.all_to_all(log_sums, "ctx", split_axis=1, concat_axis=1, tiled=True)
    routed_out = outputs_back.reshape(slot_total, QB, DH)[position].reshape(
        blocks, heads_here, top_picks, QB, DH
    )
    routed_lse = sums_back.reshape(slot_total, QB)[position].reshape(
        blocks, heads_here, top_picks, QB
    )
    own_keys = span_keys.reshape(blocks, QB, heads_here, DH)
    own_values = span_values.reshape(blocks, QB, heads_here, DH)
    causal = jnp.arange(QB)[:, None] >= jnp.arange(QB)[None, :]
    self_scores = (
        jnp.einsum("bqhd,bkhd->bhqk", blocked, own_keys, preferred_element_type=jnp.float32)
        * scaling
    )
    self_scores = jnp.where(causal[None, None], self_scores, -jnp.inf)
    self_out, self_lse = soft_partial(self_scores, own_values, "bhqk,bkhd->bhqd")
    all_lse = jnp.concatenate([routed_lse, self_lse[:, :, None]], axis=2)
    all_out = jnp.concatenate(
        [routed_out.astype(jnp.float32), self_out[:, :, None].astype(jnp.float32)], axis=2
    )
    highest = jnp.max(all_lse, axis=2, keepdims=True)
    merge_weights = jnp.exp(all_lse - highest)
    merge_weights = merge_weights / jnp.sum(merge_weights, axis=2, keepdims=True)
    attention = jnp.sum(merge_weights[..., None] * all_out, axis=2)
    attention = (
        attention.transpose(0, 2, 1, 3).reshape(blocks * QB, heads_here * DH).astype(jnp.bfloat16)
    )
    partial_sums = jnp.dot(attention, out_weight, preferred_element_type=jnp.float32)
    return lax.psum_scatter(partial_sums, "head", scatter_dimension=1, tiled=True).astype(
        jnp.bfloat16
    )


def solution(mesh):
    placed = (
        P(("groups", "ctx"), "head"),
        P(("groups", "ctx"), "head"),
        P(("groups", "ctx"), "head"),
        P(("groups", "ctx"), "head"),
        P(("groups", "ctx"), "head"),
        P("head", ("groups", "ctx"), None, None),
        P("head", None),
    )
    return jax.shard_map(
        on_device,
        mesh=mesh,
        in_specs=placed,
        out_specs=P(("groups", "ctx"), "head"),
        check_vma=False,
    )
```

profile of v0, /device:TPU:1, one launch (start us, length us, event | category | flops | bytes accessed | tf_op | source)
XLA Modules:
  0.0 391.4 jit_solution(3078422564545863952)
XLA Ops:
  10.0 6.4 %all-to-all-start.1 = ((s32[16,8,1]{0,2,1:T(1,128)}), s32[16,8,1]{0,2,1:T(1,128)S(1)}, u32[]{:S(2)}, u32[]{:S(2)}) async-start(s32[16,8,1]{0,2,1:T(1,128)} %copy.97), calls=%async_computation.1 | async-start | bytes 8192 | tf_op jit(solution)/shard_map/all_to_all | solution.py:80
  19.8 3.1 gather_fusion.4
  22.9 3.8 copy_select_fusion
  26.7 5.6 %all-to-all-start = ((bf16[16,8,128,128]{3,2,0,1:T(8,128)(2,1)}), bf16[16,8,128,128]{3,2,0,1:T(8,128)(2,1)}, u32[]{:S(2)}, u32[]{:S(2)}) async-start(bf16[16,8,128,128]{3,2,0,1:T(8,128)(2,1)} %copy_select_fusion), calls=%async_computation | async-start | bytes 8388608 | tf_op jit(solution)/shard_map/all_to_all | solution.py:79
  36.1 88.0 %all-to-all-done = bf16[16,8,128,128]{3,2,0,1:T(8,128)(2,1)} async-done(((bf16[16,8,128,128]{3,2,0,1:T(8,128)(2,1)}), bf16[16,8,128,128]{3,2,0,1:T(8,128)(2,1)}, u32[]{:S(2)}, u32[]{:S(2)}) %all-to-all-start) | async-done | bytes 4194336 | tf_op jit(solution)/shard_map/all_to_all | solution.py:79
  124.1 119.4 %while.13 = (s32[]{:T(128)}, bf16[16,8,128,128]{3,2,0,1:T(8,128)(2,1)}, f32[16,8,128]{2,0,1:T(8,128)S(1)}, bf16[16,8,128,128]{3,2,0,1:T(8,128)(2,1)}, s32[16,8]{...) while((s32[]{:T(128)}, bf16[16,8,128,128]{3,2,0,1:T(8,128)(2,1)}, ...), condition=%wide.region_7.8_spmd.clone, body=%wide.region_4.7_spmd.sunk.clone | while | flops 273285152 | bytes 13153525 | solution.py:76
  139.1 2.0 gather_fusion.1
  146.5 2.0 gather_fusion.1
  154.0 2.0 gather_fusion.1
  161.5 2.0 gather_fusion.1
  168.9 2.0 gather_fusion.1
  176.4 2.0 gather_fusion.1
  183.8 2.0 gather_fusion.1
  198.8 2.0 gather_fusion.1
  206.2 2.0 gather_fusion.1
  213.7 2.0 gather_fusion.1
  243.5 10.8 %all_to_all.24 = f32[16,8,128]{2,0,1:T(8,128)S(1)} all-to-all(f32[16,8,128]{2,0,1:T(8,128)S(1)} %get-tuple-element.43), channel_id=1, replica_groups=mesh['groups'=2,'ctx'=8,'head'=2] {'ctx'}, dimensions={1} | all-to-all | bytes 131072 | tf_op jit(solution)/shard_map/all_to_all | solution.py:88
  254.4 4.7 %all-to-all-start.3 = ((bf16[16,8,128,128]{3,2,0,1:T(8,128)(2,1)}), bf16[16,8,128,128]{3,2,0,1:T(8,128)(2,1)}, u32[]{:S(2)}, u32[]{:S(2)}) async-start(bf16[16,8,128,128]{3,2,0,1:T(8,128)(2,1)} %get-tuple-element.44), calls=%async_computation.3 | async-start | bytes 8388608 | tf_op jit(solution)/shard_map/all_to_all | solution.py:85
  261.9 88.7 %all-to-all-done.3 = bf16[16,8,128,128]{3,2,0,1:T(8,128)(2,1)} async-done(((bf16[16,8,128,128]{3,2,0,1:T(8,128)(2,1)}), bf16[16,8,128,128]{3,2,0,1:T(8,128)(2,1)}, u32[]{:S(2)}, u32[]{:S(2)}) %all-to-all-start.3) | async-done | bytes 4194336 | tf_op jit(solution)/shard_map/all_to_all | solution.py:85
  350.6 4.7 %copy.112 = bf16[16,8,128,128]{3,2,1,0:T(8,128)(2,1)} copy(bf16[16,8,128,128]{3,2,0,1:T(8,128)(2,1)} %all-to-all-done.3) | data formatting | bytes 8388608 | tf_op jit(solution)/shard_map/all_to_all | solution.py:85
  355.3 3.1 gather_fusion.6
  360.6 7.6 %fusion.15 = f32[256,4096]{1,0:T(8,128)} fusion(bf16[1024,4096]{1,0:T(8,128)(2,1)} %param.15, bf16[32,8,8,128]{3,2,1,0:T(8,128)(2,1)S(1)} %bitcast.116), kind=kOutput, calls=%fused_computation.36 | convolution fusion | flops 2147483648 | bytes 13107200 | tf_op jit(solution)/shard_map/dot_general | solution.py:115
  368.3 13.6 %reduce-scatter.2.cloned.1.call-done = f32[256,2048]{1,0:T(8,128)} async-done(((f32[256,4096]{1,0:T(8,128)}), f32[256,2048]{1,0:T(8,128)}) %reduce-scatter.2.cloned.1.call-update) | async-done | bytes 2097168 | tf_op jit(solution)/shard_map/reduce_scatter | solution.py:116
  381.8 2.7 convert_element_type.43
  (194 shorter events, 114.2 us)
Async XLA Ops:
  10.0 16.7 %all-to-all-start.1 = ((s32[16,8,1]{0,2,1:T(1,128)}), s32[16,8,1]{0,2,1:T(1,128)S(1)}, u32[]{:S(2)}, u32[]{:S(2)}) async-start(s32[16,8,1]{0,2,1:T(1,128)} %copy.97), calls=%async_computation.1 | async-start | bytes 8192 | tf_op jit(solution)/shard_map/all_to_all | solution.py:80
  18.9 0.8 copy-start
  26.7 5.6 %copy-start.2 = (bf16[512,1024]{1,0:T(8,128)(2,1)S(1)}, bf16[512,1024]{1,0:T(8,128)(2,1)}, u32[]{:S(2)}) copy-start(bf16[512,1024]{1,0:T(8,128)(2,1)} %param.12) | copy-start | bytes 3145732
  26.7 97.5 %all-to-all-start = ((bf16[16,8,128,128]{3,2,0,1:T(8,128)(2,1)}), bf16[16,8,128,128]{3,2,0,1:T(8,128)(2,1)}, u32[]{:S(2)}, u32[]{:S(2)}) async-start(bf16[16,8,128,128]{3,2,0,1:T(8,128)(2,1)} %copy_select_fusion), calls=%async_computation | async-start | bytes 8388608 | tf_op jit(solution)/shard_map/all_to_all | solution.py:79
  32.2 1.9 copy-start.3
  254.4 4.8 %copy-start.4 = (bf16[256,1024]{1,0:T(8,128)(2,1)S(1)}, bf16[256,1024]{1,0:T(8,128)(2,1)}, u32[]{:S(2)}) copy-start(bf16[256,1024]{1,0:T(8,128)(2,1)} %param.10) | copy-start | bytes 1572868
  254.4 4.9 %copy-start.5 = (bf16[256,1024]{1,0:T(8,128)(2,1)S(1)}, bf16[256,1024]{1,0:T(8,128)(2,1)}, u32[]{:S(2)}) copy-start(bf16[256,1024]{1,0:T(8,128)(2,1)} %param.11) | copy-start | bytes 1572868
  254.4 5.1 %copy-start.1 = (bf16[32,8,8,128]{3,2,1,0:T(8,128)(2,1)S(1)}, bf16[32,8,8,128]{3,2,1,0:T(8,128)(2,1)}, u32[]{:S(2)}) copy-start(bf16[32,8,8,128]{3,2,1,0:T(8,128)(2,1)} %copy-done) | copy-start | bytes 1572868
  254.4 96.2 %all-to-all-start.3 = ((bf16[16,8,128,128]{3,2,0,1:T(8,128)(2,1)}), bf16[16,8,128,128]{3,2,0,1:T(8,128)(2,1)}, u32[]{:S(2)}, u32[]{:S(2)}) async-start(bf16[16,8,128,128]{3,2,0,1:T(8,128)(2,1)} %get-tuple-element.44), calls=%async_computation.3 | async-start | bytes 8388608 | tf_op jit(solution)/shard_map/all_to_all | solution.py:85
  259.1 122.8 %reduce-scatter.2.cloned.1.call-start = ((), (), s32[]{:S(2)}) async-start(), calls=%async_computation.5 | async-start | bytes 6291456 | tf_op jit(solution)/shard_map/reduce_scatter | solution.py:116
Sparse Core Ops, SparseCore 0:
  368.4 13.4 reduce-scatter.1
where the time goes:
time: 394 us; the launch traced here: 391 us
  waiting for transfers between devices  190 us (48%)
  local copies, waits for them, and re-layouts  85.9 us (22%)
  matrix products  53.8 us (14%)
  other arithmetic  19.3 us (5%)
  starting transfers between devices  16.7 us (4%)
  between operations  13.7 us (3%)
  blocking collectives  10.8 us (3%)
    all_to_all x1, waiting for transfers between devices, on_device(): lax.all_to_all(shortened(outputs), 'ctx', split_axis=1, concat_axis=1, ti...  88.7 us
    all_to_all x1, waiting for transfers between devices, on_device(): lax.all_to_all(slot_queries, 'ctx', split_axis=1, concat_axis=1, tiled=True)  88 us
    gather x16, local copies, waits for them, and re-layouts, one_portion(): chosen_keys = keys_by_head[head_ids]  31.6 us
    gather x16, local copies, waits for them, and re-layouts, one_portion(): chosen_values = values_by_head[head_ids]  31.6 us
    dot_general x16, matrix products, one_portion(): jnp.einsum('pqd,pkd->pqk', queried, chosen_keys, preferred_element_type=j...  23.6 us
    dot_general x17, matrix products, soft_partial(): jnp.einsum(pattern, weights_low, values_block, preferred_element_type=jnp...  22.1 us
    reduce_scatter x1, waiting for transfers between devices, on_device(): lax.psum_scatter(partial_sums, 'head', scatter_dimension=1, tiled=True)  13.6 us
    all_to_all x1, blocking collectives, on_device(): lax.all_to_all(log_sums, 'ctx', split_axis=1, concat_axis=1, tiled=True)  10.8 us
  transfers between devices with their start and end apart: 4, of which 3 were waited for; matrix products, arithmetic and copies ran while one was open for 4% of the time, Pallas kernels for 0%

commit v1 on v0

--- a/solution.py
+++ b/solution.py
@@ -1,8 +1,11 @@
+import functools
 import math
 
 import jax
 import jax.numpy as jnp
 from jax import lax
+from jax.experimental import pallas as pl
+from jax.experimental.pallas import tpu as pltpu
 from jax.sharding import PartitionSpec as P
 
 DH = 128
@@ -29,7 +32,7 @@
     return (result, log_total)
 
 
-def on_device(queries, span_keys, span_values, cache_keys, cache_values, routes, out_weight):
+def routed_by_slots(queries, span_keys, span_values, cache_keys, cache_values, routes, out_weight):
     blocks = routes.shape[1]
     heads_here = routes.shape[2]
     top_picks = routes.shape[3]
@@ -118,6 +121,441 @@
     )
 
 
+BIG = 1e30
+LOG2E = math.log2(math.e)
+EXTRA = 16
+
+
+def packed_rows(out, lse):
+    high = lse.astype(jnp.bfloat16)
+    rest = lse - high.astype(jnp.float32)
+    middle = rest.astype(jnp.bfloat16)
+    low = (rest - middle.astype(jnp.float32)).astype(jnp.bfloat16)
+    row = lax.broadcasted_iota(jnp.int32, (EXTRA, lse.shape[1]), 0)
+    tail = jnp.where(
+        row == 0,
+        high.astype(jnp.float32),
+        jnp.where(
+            row == 1,
+            middle.astype(jnp.float32),
+            jnp.where(row == 2, low.astype(jnp.float32), 0.0),
+        ),
+    )
+    return out.astype(jnp.bfloat16), tail.astype(jnp.bfloat16)
+
+
+def store_message(ref, out, lse):
+    body, tail = packed_rows(out, lse)
+    ref[0:DH, :] = body
+    ref[DH : DH + EXTRA, :] = tail
+
+
+def load_message(ref):
+    out = ref[0:DH, :].astype(jnp.float32)
+    lse = jnp.sum(ref[DH : DH + EXTRA, :].astype(jnp.float32), axis=0, keepdims=True)
+    return out, lse
+
+
+def merged(first, second):
+    out_a, lse_a = first
+    out_b, lse_b = second
+    top = jnp.maximum(lse_a, lse_b)
+    weight_a = jnp.exp2(lse_a - top)
+    weight_b = jnp.exp2(lse_b - top)
+    total = weight_a + weight_b
+    return (
+        out_a * (weight_a / total) + out_b * (weight_b / total),
+        top + jnp.log2(total),
+    )
+
+
+def kernel(
+    stages,
+    heads,
+    blocks,
+    q_ref,
+    flag_ref,
+    span_k,
+    span_v,
+    k_ref,
+    v_ref,
+    w_hbm,
+    y_ref,
+    qg,
+    kr,
+    vr,
+    part,
+    from_left,
+    from_right,
+    selfp,
+    att,
+    wv,
+    ag_send,
+    ag_recv,
+    rs_send,
+    rs_recv,
+    kv_send,
+    kv_recv,
+    att_send,
+    att_recv,
+    w_sem,
+):
+    rows = blocks * QB
+    span = k_ref.shape[0]
+    width = heads * DH
+    columns = y_ref.shape[1]
+    me = lax.axis_index("ctx")
+    core = lax.axis_index("head")
+    z = me // 2
+    y = me % 2
+    pair = me + 1 - 2 * y
+    other = 1 - core
+    has_left = z > 0
+    has_right = z < stages - 1
+    scale = LOG2E / math.sqrt(DH)
+
+    def head_columns(h):
+        return pl.ds(pl.multiple_of(h * DH, DH), DH)
+
+    barrier = pltpu.get_barrier_semaphore()
+    pl.semaphore_signal(barrier, inc=1, device_id={"ctx": pair})
+    pl.semaphore_signal(barrier, inc=1, device_id={"head": other})
+
+    @pl.when(has_left)
+    def _():
+        pl.semaphore_signal(barrier, inc=1, device_id={"ctx": me - 2})
+
+    @pl.when(has_right)
+    def _():
+        pl.semaphore_signal(barrier, inc=1, device_id={"ctx": me + 2})
+
+    for h in range(heads):
+        qg[z, h, 0:rows, :] = q_ref[:, h * DH : (h + 1) * DH]
+        qg[z, h, rows:, :] = flag_ref[h]
+
+    pl.semaphore_wait(
+        barrier, 2 + jnp.minimum(z, 1) + jnp.minimum(stages - 1 - z, 1)
+    )
+
+    def kv_copies(h):
+        return (
+            pltpu.make_async_remote_copy(
+                src_ref=k_ref.at[:, head_columns(h)],
+                dst_ref=kr.at[h],
+                send_sem=kv_send.at[0, h],
+                recv_sem=kv_recv.at[0, h],
+                device_id={"ctx": pair},
+            ),
+            pltpu.make_async_remote_copy(
+                src_ref=v_ref.at[:, head_columns(h)],
+                dst_ref=vr.at[h],
+                send_sem=kv_send.at[1, h],
+                recv_sem=kv_recv.at[1, h],
+                device_id={"ctx": pair},
+            ),
+        )
+
+    def ag_copy(h, source, step):
+        return pltpu.make_async_remote_copy(
+            src_ref=qg.at[source, h],
+            dst_ref=qg.at[source, h],
+            send_sem=ag_send.at[(step + 1) // 2, h, source],
+            recv_sem=ag_recv.at[h, source],
+            device_id={"ctx": me + 2 * step},
+        )
+
+    def rs_copy(h, dest, step):
+        return pltpu.make_async_remote_copy(
+            src_ref=part.at[h, dest],
+            dst_ref=(from_left if step > 0 else from_right).at[h, dest],
+            send_sem=rs_send.at[h, dest],
+            recv_sem=rs_recv.at[(step + 1) // 2, h, dest],
+            device_id={"ctx": me + 2 * step},
+        )
+
+    def att_copy(h):
+        place = pl.ds(pl.multiple_of(core * width + h * DH, DH), DH)
+        return pltpu.make_async_remote_copy(
+            src_ref=att.at[:, place],
+            dst_ref=att.at[:, place],
+            send_sem=att_send.at[h],
+            recv_sem=att_recv.at[h],
+            device_id={"head": other},
+        )
+
+    w_rows = pl.ds(pl.multiple_of(core * width, DH), width)
+    w_remote = pltpu.make_async_remote_copy(
+        src_ref=w_hbm.at[:, pl.ds(pl.multiple_of(other * columns, DH), columns)],
+        dst_ref=wv.at[w_rows, :],
+        send_sem=w_sem.at[0],
+        recv_sem=w_sem.at[1],
+        device_id={"head": other},
+    )
+    w_local = pltpu.make_async_copy(
+        w_hbm.at[:, pl.ds(pl.multiple_of(core * columns, DH), columns)],
+        wv.at[w_rows, :],
+        w_sem.at[2],
+    )
+
+    @pl.loop(0, heads)
+    def _(h):
+        for copy in kv_copies(h):
+            copy.start()
+
+    def gather_step(t):
+        for a in range(stages):
+            h = t - a
+
+            @pl.when((h >= 0) & (h < heads))
+            def _():
+                for step in (1, -1):
+                    source = z - a * step
+                    here = (source >= 0) & (source < stages)
+                    onward = has_right if step > 0 else has_left
+
+                    @pl.when(here)
+                    def _():
+                        if a > 0:
+                            ag_copy(h, source, step).wait_recv()
+
+                        @pl.when(onward)
+                        def _():
+                            ag_copy(h, source, step).start()
+
+    def compute(h):
+        for copy in kv_copies(h):
+            copy.wait_recv()
+        keys = (k_ref.at[:, head_columns(h)], kr.at[h])
+        values_t = (v_ref[:, head_columns(h)].T, vr[h].T)
+
+        @pl.loop(0, stages)
+        def _(s):
+            queried = qg[s, h, 0:rows, :]
+            flags = qg[s, h, rows:, :].astype(jnp.float32)
+            row = lax.broadcasted_iota(jnp.int32, flags.shape, 0)
+            routed, scores, highest = [], [], None
+            for at, number in enumerate((me, pair)):
+                chosen = jnp.concatenate(
+                    [
+                        jnp.sum(
+                            jnp.where(row == number * blocks + j, flags, 0.0),
+                            axis=0,
+                            keepdims=True,
+                        )
+                        for j in range(blocks)
+                    ],
+                    axis=1,
+                )
+                score = lax.dot_general(
+                    keys[at][...],
+                    queried,
+                    (((1,), (1,)), ((), ())),
+                    preferred_element_type=jnp.float32,
+                )
+                top = jnp.where(
+                    chosen > 0.0, jnp.max(score, axis=0, keepdims=True) * scale, -BIG
+                )
+                highest = top if highest is None else jnp.maximum(highest, top)
+                routed.append(chosen)
+                scores.append(score)
+            total, out = None, None
+            for at in range(2):
+                shift = jnp.where(routed[at] > 0.0, highest, BIG)
+                exponent = jnp.exp2(scores[at] * scale - shift)
+                portion = jnp.sum(exponent, axis=0, keepdims=True)
+                result = jnp.dot(
+                    values_t[at],
+                    exponent.astype(jnp.bfloat16),
+                    preferred_element_type=jnp.float32,
+                )
+                total = portion if total is None else total + portion
+                out = result if out is None else out + result
+            safe = jnp.maximum(total, 0.5)
+            store_message(
+                part.at[h, s],
+                out * (1.0 / safe),
+                jnp.where(total > 0.0, highest + jnp.log2(safe), -BIG),
+            )
+
+    def self_part(h):
+        for j in range(blocks):
+            here = pl.ds(j * QB, QB)
+            score = lax.dot_general(
+                span_k[here, head_columns(h)],
+                q_ref[here, head_columns(h)],
+                (((1,), (1,)), ((), ())),
+                preferred_element_type=jnp.float32,
+            )
+            shape = (QB, QB)
+            causal = lax.broadcasted_iota(jnp.int32, shape, 0) <= lax.broadcasted_iota(
+                jnp.int32, shape, 1
+            )
+            score = jnp.where(causal, score * scale, -BIG)
+            top = jnp.max(score, axis=0, keepdims=True)
+            exponent = jnp.exp2(score - top)
+            total = jnp.sum(exponent, axis=0, keepdims=True)
+            out = jnp.dot(
+                span_v[here, head_columns(h)].T,
+                exponent.astype(jnp.bfloat16),
+                preferred_element_type=jnp.float32,
+            )
+            store_message(
+                selfp.at[h, :, j * QB : (j + 1) * QB], out * (1.0 / total), top + jnp.log2(total)
+            )
+
+    def reduce_step(h, step):
+        arrived = from_left if step > 0 else from_right
+        first = ~has_left if step > 0 else ~has_right
+
+        @pl.when((h >= 0) & (h < heads))
+        def _():
+            for dest in range(stages):
+                ahead = (dest - z) * step
+
+                @pl.when((ahead >= 0) & ~first)
+                def _():
+                    rs_copy(h, dest, step).wait_recv()
+                    store_message(
+                        part.at[h, dest],
+                        *merged(
+                            load_message(part.at[h, dest]), load_message(arrived.at[h, dest])
+                        ),
+                    )
+
+                @pl.when(ahead > 0)
+                def _():
+                    rs_copy(h, dest, step).start()
+
+    def finish(h):
+        out, _ = merged(load_message(part.at[h, z]), load_message(selfp.at[h]))
+        place = pl.ds(pl.multiple_of(core * width + h * DH, DH), DH)
+        att[:, place] = out.T.astype(jnp.bfloat16)
+        att_copy(h).start()
+
+    gather_step(0)
+    w_remote.start()
+    w_local.start()
+
+    @pl.loop(0, heads)
+    def _(h):
+        self_part(h)
+
+    last = stages - 1
+
+    @pl.loop(1, heads + 2 * last + 1)
+    def _(t):
+        gather_step(t)
+
+        @pl.when((t >= last) & (t < heads + last))
+        def _():
+            compute(t - last)
+
+        reduce_step(t - last - z, 1)
+        reduce_step(t - 2 * last + z, -1)
+
+        @pl.when((t >= 2 * last) & (t < heads + 2 * last))
+        def _():
+            finish(t - 2 * last)
+
+    w_local.wait()
+    w_remote.wait()
+
+    @pl.loop(0, heads)
+    def _(h):
+        att_copy(h).wait_recv()
+
+    tile = math.gcd(columns, 512)
+
+    @pl.loop(0, columns // tile)
+    def _(n):
+        here = pl.ds(pl.multiple_of(n * tile, tile), tile)
+        y_ref[:, here] = jnp.dot(
+            att[...], wv[:, here], preferred_element_type=jnp.float32
+        ).astype(jnp.bfloat16)
+
+    @pl.loop(0, heads)
+    def _(h):
+        att_copy(h).wait_send()
+        for copy in kv_copies(h):
+            copy.wait_send()
+        for other_z in range(stages):
+
+            @pl.when((other_z <= z) & has_right)
+            def _():
+                ag_copy(h, other_z, 1).wait_send()
+
+            @pl.when((other_z >= z) & has_left)
+            def _():
+                ag_copy(h, other_z, -1).wait_send()
+
+            @pl.when(other_z > z)
+            def _():
+                rs_copy(h, other_z, 1).wait_send()
+
+            @pl.when(other_z < z)
+            def _():
+                rs_copy(h, other_z, -1).wait_send()
+
+
+def routed_by_lines(queries, span_keys, span_values, cache_keys, cache_values, routes, out_weight):
+    blocks, heads = routes.shape[1:3]
+    devices = lax.axis_size("ctx")
+    stages = devices // 2
+    rows = blocks * QB
+    span = cache_keys.shape[0]
+    columns = out_weight.shape[1] // lax.axis_size("head")
+    named = jnp.any(
+        routes[0][None] == jnp.arange(devices, dtype=jnp.int32)[:, None, None, None], axis=-1
+    )
+    flags = named.transpose(2, 0, 1).reshape(heads, devices * blocks).astype(jnp.bfloat16)
+    tail = devices * blocks
+    flags = jnp.broadcast_to(flags[:, :, None], (heads, tail, DH))
+    vmem = pl.BlockSpec(memory_space=pltpu.VMEM)
+    message = (heads, stages, DH + EXTRA, rows)
+    dma = pltpu.SemaphoreType.DMA
+    return pl.pallas_call(
+        functools.partial(kernel, stages, heads, blocks),
+        out_shape=jax.ShapeDtypeStruct((rows, columns), jnp.bfloat16),
+        in_specs=[vmem] * 6 + [pl.BlockSpec(memory_space=pl.ANY)],
+        out_specs=vmem,
+        scratch_shapes=[
+            pltpu.VMEM((stages, heads, rows + tail, DH), jnp.bfloat16),
+            pltpu.VMEM((heads, span, DH), jnp.bfloat16),
+            pltpu.VMEM((heads, span, DH), jnp.bfloat16),
+            pltpu.VMEM(message, jnp.bfloat16),
+            pltpu.VMEM(message, jnp.bfloat16),
+            pltpu.VMEM(message, jnp.bfloat16),
+            pltpu.VMEM((heads, DH + EXTRA, rows), jnp.bfloat16),
+            pltpu.VMEM((rows, 2 * heads * DH), jnp.bfloat16),
+            pltpu.VMEM((2 * heads * DH, columns), jnp.bfloat16),
+            dma((2, heads, stages)),
+            dma((heads, stages)),
+            dma((heads, stages)),
+            dma((2, heads, stages)),
+            dma((2, heads)),
+            dma((2, heads)),
+            dma((heads,)),
+            dma((heads,)),
+            dma((3,)),
+        ],
+        compiler_params=pltpu.CompilerParams(
+            collective_id=0, has_side_effects=True, vmem_limit_bytes=60 * 2**20
+        ),
+        cost_estimate=pl.CostEstimate(
+            flops=8 * stages * heads * rows * span * DH, bytes_accessed=2**24, transcendentals=0
+        ),
+    )(queries, flags, span_keys, span_values, cache_keys, cache_values, out_weight)
+
+
+def on_device(queries, span_keys, span_values, cache_keys, cache_values, routes, out_weight):
+    blocks, heads, top_picks = routes.shape[1:]
+    devices = lax.axis_size("ctx")
+    arguments = (queries, span_keys, span_values, cache_keys, cache_values, routes, out_weight)
+    slots = max(2, 2 * blocks * heads * top_picks // devices)
+    dense = slots >= blocks * heads and devices % 2 == 0 and lax.axis_size("head") == 2
+    return (routed_by_lines if dense else routed_by_slots)(*arguments)
+
+
 def solution(mesh):
     placed = (
         P(("groups", "ctx"), "head"),

time: 394 us -> 86.8 us (0.22)
  waiting for transfers between devices: 190 us -> 0 us
  local copies, waits for them, and re-layouts: 85.9 us -> 3.1 us
  Pallas kernels: 0 us -> 82.8 us
  matrix products: 53.8 us -> 0 us
  other arithmetic: 19.3 us -> 0.7 us
  starting transfers between devices: 16.7 us -> 0 us
  between operations: 13.7 us -> 0.01 us
  blocking collectives: 10.8 us -> 0 us
    all_to_all x3 -> x0, waiting for transfers between devices: 177 us -> none  [the longest x1 88.7 us: on_device(): lax.all_to_all(shortened(outputs), 'ctx', split_axis=1, concat_axis=1, ti...]
    pallas_call x0 -> x1, Pallas kernels: none -> 82.8 us  [routed_by_lines(): pl.pallas_call(functools.partial(kernel, stages, heads, blocks), out_shap...]
    gather x37 -> x0, local copies, waits for them, and re-layouts: 72.4 us -> none  [the longest x16 31.6 us: one_portion(): chosen_keys = keys_by_head[head_ids]]
    dot_general x35 -> x0, matrix products: 53.8 us -> none  [the longest x16 23.6 us: one_portion(): jnp.einsum('pqd,pkd->pqk', queried, chosen_keys, preferred_element_type=j...]
    all_to_all x3 -> x0, starting transfers between devices: 16.6 us -> none  [the longest x1 6.37 us: on_device(): lax.all_to_all(slot_heads, 'ctx', split_axis=1, concat_axis=1, tiled=True)]
    reduce_scatter x1 -> x0, waiting for transfers between devices: 13.6 us -> none  [on_device(): lax.psum_scatter(partial_sums, 'head', scatter_dimension=1, tiled=True)]
    reduce_sum x20 -> x0, other arithmetic: 11.5 us -> none  [the longest x17 9.44 us: soft_partial(): denominator = jnp.sum(exponent, axis=-1, keepdims=True)]
    all_to_all x1 -> x0, blocking collectives: 10.8 us -> none  [on_device(): lax.all_to_all(log_sums, 'ctx', split_axis=1, concat_axis=1, tiled=True)]
  transfers between devices with their start and end apart: 4 -> 0, of which waited for: 3 -> 0; matrix products, arithmetic and copies ran while one was open for 4% -> 0% of each run, Pallas kernels for 0% -> 0%
where the time goes in v1:
time: 86.8 us; the launch traced here: 86.7 us
  Pallas kernels  82.8 us (95%)
  local copies, waits for them, and re-layouts  3.1 us (4%)
    pallas_call x1, Pallas kernels, routed_by_lines(): pl.pallas_call(functools.partial(kernel, stages, heads, blocks), out_shap...  82.8 us
    unnamed x1, local copies, waits for them, and re-layouts  2.3 us

profile of v1, /device:TPU:1, one launch (start us, length us, event | category | flops | bytes accessed | tf_op | source)
XLA Modules:
  0.0 86.7 jit_solution(16590081253421120691)
XLA Ops:
  0.0 0.7 fusion
  0.7 0.1 copy.11
  0.8 0.7 broadcast_in_dim.2.flag_ref
  1.5 82.8 %shard_map.73 = bf16[256,2048]{1,0:T(8,128)(2,1)} custom-call(bf16[256,1024]{1,0:T(8,128)(2,1)} %q_ref.1, bf16[8,16,128]{2,1,0:T(8,128)(2,1)} %broadcast_in_dim.2.flag_ref, bf16[256,1024]{1,0:T(8,128)(2,1)} %span_k.1, bf16[256,1024]{1,0:T(8,128)(2,1)} %span_v.1, bf16[512,1024]{1,0:T(8,128)(2,1)} %k_ref.1, bf16[512,1024]{1,0:T(8,128)(2,1)} %v_ref.1, ...), custom_call_target="tpu_custom_call" | custom-call | flops 4294967296 | bytes 16777216 | tf_op jit(solution)/shard_map/pallas_call | solution.py:516
  84.4 2.3 %copy.13 = bf16[256,2048]{1,0:T(8,128)(2,1)} copy(bf16[256,2048]{1,0:T(8,128)(2,1)} %shard_map.73) | data formatting | bytes 2097152
  (2 shorter events, 0.0 us)

commit v2 on v1

--- a/solution.py
+++ b/solution.py
@@ -123,37 +123,17 @@
 
 BIG = 1e30
 LOG2E = math.log2(math.e)
-EXTRA = 16
-
-
-def packed_rows(out, lse):
-    high = lse.astype(jnp.bfloat16)
-    rest = lse - high.astype(jnp.float32)
-    middle = rest.astype(jnp.bfloat16)
-    low = (rest - middle.astype(jnp.float32)).astype(jnp.bfloat16)
-    row = lax.broadcasted_iota(jnp.int32, (EXTRA, lse.shape[1]), 0)
-    tail = jnp.where(
-        row == 0,
-        high.astype(jnp.float32),
-        jnp.where(
-            row == 1,
-            middle.astype(jnp.float32),
-            jnp.where(row == 2, low.astype(jnp.float32), 0.0),
-        ),
-    )
-    return out.astype(jnp.bfloat16), tail.astype(jnp.bfloat16)
-
-
-def store_message(ref, out, lse):
-    body, tail = packed_rows(out, lse)
-    ref[0:DH, :] = body
-    ref[DH : DH + EXTRA, :] = tail
-
-
-def load_message(ref):
-    out = ref[0:DH, :].astype(jnp.float32)
-    lse = jnp.sum(ref[DH : DH + EXTRA, :].astype(jnp.float32), axis=0, keepdims=True)
-    return out, lse
+LANES = 128
+VALUE_ROWS = DH + 16
+
+
+def store_partial(ref, lse_ref, out, lse):
+    ref[...] = out.astype(jnp.bfloat16)
+    lse_ref[...] = lse
+
+
+def load_partial(ref, lse_ref):
+    return ref[...].astype(jnp.float32), lse_ref[...]
 
 
 def merged(first, second):
@@ -184,16 +164,25 @@
     qg,
     kr,
     vr,
+    fg,
+    chosen_rows,
     part,
-    from_left,
-    from_right,
+    part_lse,
+    arrived,
+    arrived_lse,
     selfp,
+    self_lse,
+    vt,
     att,
     wv,
     ag_send,
     ag_recv,
+    flag_send,
+    flag_recv,
     rs_send,
     rs_recv,
+    lse_send,
+    lse_recv,
     kv_send,
     kv_recv,
     att_send,
@@ -210,6 +199,7 @@
     y = me % 2
     pair = me + 1 - 2 * y
     other = 1 - core
+    last = stages - 1
     has_left = z > 0
     has_right = z < stages - 1
     scale = LOG2E / math.sqrt(DH)
@@ -230,8 +220,8 @@
         pl.semaphore_signal(barrier, inc=1, device_id={"ctx": me + 2})
 
     for h in range(heads):
-        qg[z, h, 0:rows, :] = q_ref[:, h * DH : (h + 1) * DH]
-        qg[z, h, rows:, :] = flag_ref[h]
+        qg[z, h] = q_ref[:, h * DH : (h + 1) * DH]
+    fg[z] = flag_ref[...]
 
     pl.semaphore_wait(
         barrier, 2 + jnp.minimum(z, 1) + jnp.minimum(stages - 1 - z, 1)
@@ -264,13 +254,32 @@
             device_id={"ctx": me + 2 * step},
         )
 
-    def rs_copy(h, dest, step):
+    def flag_copy(source, step):
         return pltpu.make_async_remote_copy(
-            src_ref=part.at[h, dest],
-            dst_ref=(from_left if step > 0 else from_right).at[h, dest],
-            send_sem=rs_send.at[h, dest],
-            recv_sem=rs_recv.at[(step + 1) // 2, h, dest],
+            src_ref=fg.at[source],
+            dst_ref=fg.at[source],
+            send_sem=flag_send.at[(step + 1) // 2, source],
+            recv_sem=flag_recv.at[source],
             device_id={"ctx": me + 2 * step},
+        )
+
+    def rs_copies(h, dest, step):
+        side = (step + 1) // 2
+        return (
+            pltpu.make_async_remote_copy(
+                src_ref=part.at[h, dest],
+                dst_ref=arrived.at[side, h, dest],
+                send_sem=rs_send.at[h, dest],
+                recv_sem=rs_recv.at[side, h, dest],
+                device_id={"ctx": me + 2 * step},
+            ),
+            pltpu.make_async_remote_copy(
+                src_ref=part_lse.at[h, dest],
+                dst_ref=arrived_lse.at[side, h, dest],
+                send_sem=lse_send.at[h, dest],
+                recv_sem=lse_recv.at[side, h, dest],
+                device_id={"ctx": me + 2 * step},
+            ),
         )
 
     def att_copy(h):
@@ -297,13 +306,24 @@
         w_sem.at[2],
     )
 
-    @pl.loop(0, heads)
-    def _(h):
-        for copy in kv_copies(h):
-            copy.start()
+    def lead(step):
+        return 2 * (last - z if step > 0 else z)
+
+    def send_own(h, step):
+        onward = has_right if step > 0 else has_left
+
+        @pl.when((h < heads) & onward)
+        def _():
+            ag_copy(h, z, step).start()
+
+        @pl.when((h == 0) & onward)
+        def _():
+            flag_copy(z, step).start()
 
     def gather_step(t):
-        for a in range(stages):
+        for step in (1, -1):
+            send_own(t + lead(step), step)
+        for a in range(1, stages):
             h = t - a
 
             @pl.when((h >= 0) & (h < heads))
@@ -315,67 +335,73 @@
 
                     @pl.when(here)
                     def _():
-                        if a > 0:
-                            ag_copy(h, source, step).wait_recv()
+                        ag_copy(h, source, step).wait_recv()
 
                         @pl.when(onward)
                         def _():
                             ag_copy(h, source, step).start()
 
-    def compute(h):
+                        @pl.when(h == 0)
+                        def _():
+                            flag_copy(source, step).wait_recv()
+
+                            @pl.when(onward)
+                            def _():
+                                flag_copy(source, step).start()
+
+    def read_flags():
+        for s in range(stages):
+            flags = fg[s].astype(jnp.float32)
+            lane = lax.broadcasted_iota(jnp.int32, flags.shape, 1)
+            for at, number in enumerate((me, pair)):
+                chosen = jnp.sum(
+                    jnp.where(lane == number, flags, 0.0), axis=1, keepdims=True
+                )
+                chosen_rows[s, at] = jnp.broadcast_to(chosen, flags.shape)
+
+    def prepare(h):
         for copy in kv_copies(h):
             copy.wait_recv()
+        filler = jnp.ones((VALUE_ROWS - DH, span), jnp.bfloat16)
+        for at, value in enumerate((v_ref[:, head_columns(h)], vr[h])):
+            vt[at, 0:DH, :] = value.T
+            vt[at, DH:VALUE_ROWS, :] = filler
+
+    def compute(h, s):
         keys = (k_ref.at[:, head_columns(h)], kr.at[h])
-        values_t = (v_ref[:, head_columns(h)].T, vr[h].T)
-
-        @pl.loop(0, stages)
-        def _(s):
-            queried = qg[s, h, 0:rows, :]
-            flags = qg[s, h, rows:, :].astype(jnp.float32)
-            row = lax.broadcasted_iota(jnp.int32, flags.shape, 0)
-            routed, scores, highest = [], [], None
-            for at, number in enumerate((me, pair)):
-                chosen = jnp.concatenate(
-                    [
-                        jnp.sum(
-                            jnp.where(row == number * blocks + j, flags, 0.0),
-                            axis=0,
-                            keepdims=True,
-                        )
-                        for j in range(blocks)
-                    ],
-                    axis=1,
-                )
-                score = lax.dot_general(
-                    keys[at][...],
-                    queried,
-                    (((1,), (1,)), ((), ())),
-                    preferred_element_type=jnp.float32,
-                )
-                top = jnp.where(
-                    chosen > 0.0, jnp.max(score, axis=0, keepdims=True) * scale, -BIG
-                )
-                highest = top if highest is None else jnp.maximum(highest, top)
-                routed.append(chosen)
-                scores.append(score)
-            total, out = None, None
-            for at in range(2):
-                shift = jnp.where(routed[at] > 0.0, highest, BIG)
-                exponent = jnp.exp2(scores[at] * scale - shift)
-                portion = jnp.sum(exponent, axis=0, keepdims=True)
-                result = jnp.dot(
-                    values_t[at],
-                    exponent.astype(jnp.bfloat16),
-                    preferred_element_type=jnp.float32,
-                )
-                total = portion if total is None else total + portion
-                out = result if out is None else out + result
-            safe = jnp.maximum(total, 0.5)
-            store_message(
-                part.at[h, s],
-                out * (1.0 / safe),
-                jnp.where(total > 0.0, highest + jnp.log2(safe), -BIG),
+        queried = qg[s, h]
+        routed, scores, highest = [], [], None
+        for at in range(2):
+            chosen = jnp.concatenate(
+                [chosen_rows[s, at, pl.ds(h * blocks + j, 1), :] for j in range(blocks)],
+                axis=1,
             )
+            score = lax.dot_general(
+                keys[at][...],
+                queried,
+                (((1,), (1,)), ((), ())),
+                preferred_element_type=jnp.float32,
+            )
+            top = jnp.where(
+                chosen > 0.0, jnp.max(score, axis=0, keepdims=True) * scale, -BIG
+            )
+            highest = top if highest is None else jnp.maximum(highest, top)
+            routed.append(chosen)
+            scores.append(score)
+        result = None
+        for at in range(2):
+            shift = jnp.where(routed[at] > 0.0, highest, BIG)
+            exponent = jnp.exp2(scores[at] * scale - shift).astype(jnp.bfloat16)
+            product = jnp.dot(vt[at], exponent, preferred_element_type=jnp.float32)
+            result = product if result is None else result + product
+        total = result[DH : DH + 1, :]
+        safe = jnp.maximum(total, 0.5)
+        store_partial(
+            part.at[h, s],
+            part_lse.at[h, s],
+            result[0:DH, :] * (1.0 / safe),
+            jnp.where(total > 0.0, highest + jnp.log2(safe), -BIG),
+        )
 
     def self_part(h):
         for j in range(blocks):
@@ -399,40 +425,62 @@
                 exponent.astype(jnp.bfloat16),
                 preferred_element_type=jnp.float32,
             )
-            store_message(
-                selfp.at[h, :, j * QB : (j + 1) * QB], out * (1.0 / total), top + jnp.log2(total)
+            store_partial(
+                selfp.at[h, :, j * QB : (j + 1) * QB],
+                self_lse.at[h, :, j * QB : (j + 1) * QB],
+                out * (1.0 / total),
+                top + jnp.log2(total),
             )
 
     def reduce_step(h, step):
-        arrived = from_left if step > 0 else from_right
+        side = (step + 1) // 2
         first = ~has_left if step > 0 else ~has_right
 
         @pl.when((h >= 0) & (h < heads))
         def _():
-            for dest in range(stages):
+            for dest in reversed(range(stages)) if step > 0 else range(stages):
                 ahead = (dest - z) * step
 
                 @pl.when((ahead >= 0) & ~first)
                 def _():
-                    rs_copy(h, dest, step).wait_recv()
-                    store_message(
-                        part.at[h, dest],
+                    for copy in rs_copies(h, dest, step):
+                        copy.wait_recv()
+                    mine = (part.at[h, dest], part_lse.at[h, dest])
+                    store_partial(
+                        *mine,
                         *merged(
-                            load_message(part.at[h, dest]), load_message(arrived.at[h, dest])
+                            load_partial(*mine),
+                            load_partial(
+                                arrived.at[side, h, dest], arrived_lse.at[side, h, dest]
+                            ),
                         ),
                     )
 
                 @pl.when(ahead > 0)
                 def _():
-                    rs_copy(h, dest, step).start()
+                    for copy in rs_copies(h, dest, step):
+                        copy.start()
 
     def finish(h):
-        out, _ = merged(load_message(part.at[h, z]), load_message(selfp.at[h]))
+        out, _ = merged(
+            load_partial(part.at[h, z], part_lse.at[h, z]),
+            load_partial(selfp.at[h], self_lse.at[h]),
+        )
         place = pl.ds(pl.multiple_of(core * width + h * DH, DH), DH)
         att[:, place] = out.T.astype(jnp.bfloat16)
         att_copy(h).start()
 
-    gather_step(0)
+    for step in (1, -1):
+
+        @pl.loop(0, lead(step) + 1)
+        def _(h):
+            send_own(h, step)
+
+    @pl.loop(0, heads)
+    def _(h):
+        for copy in kv_copies(h):
+            copy.start()
+
     w_remote.start()
     w_local.start()
 
@@ -440,22 +488,28 @@
     def _(h):
         self_part(h)
 
-    last = stages - 1
-
     @pl.loop(1, heads + 2 * last + 1)
     def _(t):
         gather_step(t)
-
-        @pl.when((t >= last) & (t < heads + last))
-        def _():
-            compute(t - last)
-
-        reduce_step(t - last - z, 1)
-        reduce_step(t - 2 * last + z, -1)
-
-        @pl.when((t >= 2 * last) & (t < heads + 2 * last))
-        def _():
-            finish(t - 2 * last)
+        h = t - last
+        busy = (h >= 0) & (h < heads)
+
+        @pl.when(h == 0)
+        def _():
+            read_flags()
+
+        @pl.when(busy)
+        def _():
+            prepare(h)
+            for s in range(stages):
+                compute(h, s)
+
+        reduce_step(h - z, 1)
+        reduce_step(h - last + z, -1)
+
+        @pl.when((h >= last) & (h < heads + last))
+        def _():
+            finish(h - last)
 
     w_local.wait()
     w_remote.wait()
@@ -488,13 +542,22 @@
             def _():
                 ag_copy(h, other_z, -1).wait_send()
 
-            @pl.when(other_z > z)
-            def _():
-                rs_copy(h, other_z, 1).wait_send()
-
-            @pl.when(other_z < z)
-            def _():
-                rs_copy(h, other_z, -1).wait_send()
+            for step in (1, -1):
+
+                @pl.when((other_z - z) * step > 0)
+                def _():
+                    for copy in rs_copies(h, other_z, step):
+                        copy.wait_send()
+
+    for other_z in range(stages):
+
+        @pl.when((other_z <= z) & has_right)
+        def _():
+            flag_copy(other_z, 1).wait_send()
+
+        @pl.when((other_z >= z) & has_left)
+        def _():
+            flag_copy(other_z, -1).wait_send()
 
 
 def routed_by_lines(queries, span_keys, span_values, cache_keys, cache_values, routes, out_weight):
@@ -507,11 +570,9 @@
     named = jnp.any(
         routes[0][None] == jnp.arange(devices, dtype=jnp.int32)[:, None, None, None], axis=-1
     )
-    flags = named.transpose(2, 0, 1).reshape(heads, devices * blocks).astype(jnp.bfloat16)
-    tail = devices * blocks
-    flags = jnp.broadcast_to(flags[:, :, None], (heads, tail, DH))
+    flags = named.transpose(2, 1, 0).reshape(heads * blocks, devices).astype(jnp.bfloat16)
+    flags = jnp.pad(flags, ((0, 0), (0, LANES - devices)))
     vmem = pl.BlockSpec(memory_space=pltpu.VMEM)
-    message = (heads, stages, DH + EXTRA, rows)
     dma = pltpu.SemaphoreType.DMA
     return pl.pallas_call(
         functools.partial(kernel, stages, heads, blocks),
@@ -519,17 +580,26 @@
         in_specs=[vmem] * 6 + [pl.BlockSpec(memory_space=pl.ANY)],
         out_specs=vmem,
         scratch_shapes=[
-            pltpu.VMEM((stages, heads, rows + tail, DH), jnp.bfloat16),
+            pltpu.VMEM((stages, heads, rows, DH), jnp.bfloat16),
             pltpu.VMEM((heads, span, DH), jnp.bfloat16),
             pltpu.VMEM((heads, span, DH), jnp.bfloat16),
-            pltpu.VMEM(message, jnp.bfloat16),
-            pltpu.VMEM(message, jnp.bfloat16),
-            pltpu.VMEM(message, jnp.bfloat16),
-            pltpu.VMEM((heads, DH + EXTRA, rows), jnp.bfloat16),
+            pltpu.VMEM((stages, heads * blocks, LANES), jnp.bfloat16),
+            pltpu.VMEM((stages, 2, heads * blocks, LANES), jnp.float32),
+            pltpu.VMEM((heads, stages, DH, rows), jnp.bfloat16),
+            pltpu.VMEM((heads, stages, 1, rows), jnp.float32),
+            pltpu.VMEM((2, heads, stages, DH, rows), jnp.bfloat16),
+            pltpu.VMEM((2, heads, stages, 1, rows), jnp.float32),
+            pltpu.VMEM((heads, DH, rows), jnp.bfloat16),
+            pltpu.VMEM((heads, 1, rows), jnp.float32),
+            pltpu.VMEM((2, VALUE_ROWS, span), jnp.bfloat16),
             pltpu.VMEM((rows, 2 * heads * DH), jnp.bfloat16),
             pltpu.VMEM((2 * heads * DH, columns), jnp.bfloat16),
             dma((2, heads, stages)),
             dma((heads, stages)),
+            dma((2, stages)),
+            dma((stages,)),
+            dma((heads, stages)),
+            dma((2, heads, stages)),
             dma((heads, stages)),
             dma((2, heads, stages)),
             dma((2, heads)),
@@ -552,7 +622,7 @@
     devices = lax.axis_size("ctx")
     arguments = (queries, span_keys, span_values, cache_keys, cache_values, routes, out_weight)
     slots = max(2, 2 * blocks * heads * top_picks // devices)
-    dense = slots >= blocks * heads and devices % 2 == 0 and lax.axis_size("head") == 2
+    dense = slots >= blocks * heads and devices % 2 == 0 and devices <= LANES and lax.axis_size("head") == 2
     return (routed_by_lines if dense else routed_by_slots)(*arguments)
 
 

time: 86.8 us -> 81.4 us (0.938)
  Pallas kernels: 82.8 us -> 77.5 us
    pallas_call x1, Pallas kernels: 82.8 us -> 77.5 us  [routed_by_lines(): pl.pallas_call(functools.partial(kernel, stages, heads, blocks), out_shap...]
where the time goes in v2:
time: 81.4 us; the launch traced here: 81.2 us
  Pallas kernels  77.5 us (95%)
  local copies, waits for them, and re-layouts  2.42 us (3%)
  other arithmetic  1.3 us (2%)
    pallas_call x1, Pallas kernels, routed_by_lines(): pl.pallas_call(functools.partial(kernel, stages, heads, blocks), out_shap...  77.5 us
    unnamed x1, local copies, waits for them, and re-layouts  2.3 us

profile of v2, /device:TPU:1, one launch (start us, length us, event | category | flops | bytes accessed | tf_op | source)
XLA Modules:
  0.0 81.2 jit_solution(15130449060860155330)
XLA Ops:
  0.0 0.7 fusion
  0.7 0.1 copy.10
  0.8 0.6 pad_convert_fusion.flag_ref
  1.4 77.5 %shard_map.73 = bf16[256,2048]{1,0:T(8,128)(2,1)} custom-call(bf16[256,1024]{1,0:T(8,128)(2,1)} %q_ref.1, bf16[16,128]{1,0:T(8,128)(2,1)} %pad_convert_fusion.flag_ref, bf16[256,1024]{1,0:T(8,128)(2,1)} %span_k.1, bf16[256,1024]{1,0:T(8,128)(2,1)} %span_v.1, bf16[512,1024]{1,0:T(8,128)(2,1)} %k_ref.1, bf16[512,1024]{1,0:T(8,128)(2,1)} %v_ref.1, ...), custom_call_target="tpu_custom_call" | custom-call | flops 4294967296 | bytes 16777216 | tf_op jit(solution)/shard_map/pallas_call | solution.py:577
  78.9 2.3 %copy.12 = bf16[256,2048]{1,0:T(8,128)(2,1)} copy(bf16[256,2048]{1,0:T(8,128)(2,1)} %shard_map.73) | data formatting | bytes 2097152
  (1 shorter events, 0.0 us)

commit v3 on v2

--- a/solution.py
+++ b/solution.py
@@ -153,12 +153,12 @@
     stages,
     heads,
     blocks,
-    q_ref,
+    q_hbm,
     flag_ref,
-    span_k,
-    span_v,
-    k_ref,
-    v_ref,
+    span_k_hbm,
+    span_v_hbm,
+    k_hbm,
+    v_hbm,
     w_hbm,
     y_ref,
     qg,
@@ -175,6 +175,10 @@
     vt,
     att,
     wv,
+    span_k,
+    span_v,
+    k_ref,
+    v_ref,
     ag_send,
     ag_recv,
     flag_send,
@@ -188,6 +192,8 @@
     att_send,
     att_recv,
     w_sem,
+    own_sem,
+    q_sem,
 ):
     rows = blocks * QB
     span = k_ref.shape[0]
@@ -219,8 +225,6 @@
     def _():
         pl.semaphore_signal(barrier, inc=1, device_id={"ctx": me + 2})
 
-    for h in range(heads):
-        qg[z, h] = q_ref[:, h * DH : (h + 1) * DH]
     fg[z] = flag_ref[...]
 
     pl.semaphore_wait(
@@ -230,14 +234,14 @@
     def kv_copies(h):
         return (
             pltpu.make_async_remote_copy(
-                src_ref=k_ref.at[:, head_columns(h)],
+                src_ref=k_hbm.at[:, head_columns(h)],
                 dst_ref=kr.at[h],
                 send_sem=kv_send.at[0, h],
                 recv_sem=kv_recv.at[0, h],
                 device_id={"ctx": pair},
             ),
             pltpu.make_async_remote_copy(
-                src_ref=v_ref.at[:, head_columns(h)],
+                src_ref=v_hbm.at[:, head_columns(h)],
                 dst_ref=vr.at[h],
                 send_sem=kv_send.at[1, h],
                 recv_sem=kv_recv.at[1, h],
@@ -245,9 +249,19 @@
             ),
         )
 
-    def ag_copy(h, source, step):
+    def q_copy(h):
+        return pltpu.make_async_copy(q_hbm.at[:, head_columns(h)], qg.at[z, h], q_sem.at[h])
+
+    own_copies = [
+        pltpu.make_async_copy(source, target, own_sem.at[i])
+        for i, (source, target) in enumerate(
+            ((k_hbm, k_ref), (v_hbm, v_ref), (span_k_hbm, span_k), (span_v_hbm, span_v))
+        )
+    ]
+
+    def ag_copy(h, source, step, own=False):
         return pltpu.make_async_remote_copy(
-            src_ref=qg.at[source, h],
+            src_ref=q_hbm.at[:, head_columns(h)] if own else qg.at[source, h],
             dst_ref=qg.at[source, h],
             send_sem=ag_send.at[(step + 1) // 2, h, source],
             recv_sem=ag_recv.at[h, source],
@@ -314,7 +328,7 @@
 
         @pl.when((h < heads) & onward)
         def _():
-            ag_copy(h, z, step).start()
+            ag_copy(h, z, step, own=True).start()
 
         @pl.when((h == 0) & onward)
         def _():
@@ -408,7 +422,7 @@
             here = pl.ds(j * QB, QB)
             score = lax.dot_general(
                 span_k[here, head_columns(h)],
-                q_ref[here, head_columns(h)],
+                qg[z, h, here, :],
                 (((1,), (1,)), ((), ())),
                 preferred_element_type=jnp.float32,
             )
@@ -432,16 +446,18 @@
                 top + jnp.log2(total),
             )
 
+    def at_end(step):
+        return ~has_left if step > 0 else ~has_right
+
     def reduce_step(h, step):
         side = (step + 1) // 2
-        first = ~has_left if step > 0 else ~has_right
-
-        @pl.when((h >= 0) & (h < heads))
+
+        @pl.when((h >= 0) & (h < heads) & ~at_end(step))
         def _():
             for dest in reversed(range(stages)) if step > 0 else range(stages):
                 ahead = (dest - z) * step
 
-                @pl.when((ahead >= 0) & ~first)
+                @pl.when(ahead >= 0)
                 def _():
                     for copy in rs_copies(h, dest, step):
                         copy.wait_recv()
@@ -486,7 +502,14 @@
 
     @pl.loop(0, heads)
     def _(h):
-        self_part(h)
+        q_copy(h).start()
+
+    for copy in own_copies:
+        copy.start()
+
+    @pl.loop(0, heads)
+    def _(h):
+        q_copy(h).wait()
 
     @pl.loop(1, heads + 2 * last + 1)
     def _(t):
@@ -497,15 +520,28 @@
         @pl.when(h == 0)
         def _():
             read_flags()
+            for copy in own_copies:
+                copy.wait()
 
         @pl.when(busy)
         def _():
             prepare(h)
-            for s in range(stages):
+            for i in range(stages):
+                s = jnp.where(2 * z >= stages, i, last - i)
                 compute(h, s)
+                for step in (1, -1):
+
+                    @pl.when(((s - z) * step > 0) & at_end(step))
+                    def _():
+                        for copy in rs_copies(h, s, step):
+                            copy.start()
 
         reduce_step(h - z, 1)
         reduce_step(h - last + z, -1)
+
+        @pl.when(busy)
+        def _():
+            self_part(h)
 
         @pl.when((h >= last) & (h < heads + last))
         def _():
@@ -573,11 +609,12 @@
     flags = named.transpose(2, 1, 0).reshape(heads * blocks, devices).astype(jnp.bfloat16)
     flags = jnp.pad(flags, ((0, 0), (0, LANES - devices)))
     vmem = pl.BlockSpec(memory_space=pltpu.VMEM)
+    anywhere = pl.BlockSpec(memory_space=pl.ANY)
     dma = pltpu.SemaphoreType.DMA
     return pl.pallas_call(
         functools.partial(kernel, stages, heads, blocks),
         out_shape=jax.ShapeDtypeStruct((rows, columns), jnp.bfloat16),
-        in_specs=[vmem] * 6 + [pl.BlockSpec(memory_space=pl.ANY)],
+        in_specs=[anywhere, vmem] + [anywhere] * 5,
         out_specs=vmem,
         scratch_shapes=[
             pltpu.VMEM((stages, heads, rows, DH), jnp.bfloat16),
@@ -594,6 +631,10 @@
             pltpu.VMEM((2, VALUE_ROWS, span), jnp.bfloat16),
             pltpu.VMEM((rows, 2 * heads * DH), jnp.bfloat16),
             pltpu.VMEM((2 * heads * DH, columns), jnp.bfloat16),
+            pltpu.VMEM((rows, heads * DH), jnp.bfloat16),
+            pltpu.VMEM((rows, heads * DH), jnp.bfloat16),
+            pltpu.VMEM((span, heads * DH), jnp.bfloat16),
+            pltpu.VMEM((span, heads * DH), jnp.bfloat16),
             dma((2, heads, stages)),
             dma((heads, stages)),
             dma((2, stages)),
@@ -607,6 +648,8 @@
             dma((heads,)),
             dma((heads,)),
             dma((3,)),
+            dma((4,)),
+            dma((heads,)),
         ],
         compiler_params=pltpu.CompilerParams(
             collective_id=0, has_side_effects=True, vmem_limit_bytes=60 * 2**20

time: 81.4 us -> 80.8 us (level)
  no operation moved by 1% of the time
where the time goes in v3:
time: 80.8 us; the launch traced here: 80.6 us
  Pallas kernels  76.9 us (95%)
  local copies, waits for them, and re-layouts  2.42 us (3%)
  other arithmetic  1.3 us (2%)
    pallas_call x1, Pallas kernels, routed_by_lines(): pl.pallas_call(functools.partial(kernel, stages, heads, blocks), out_shap...  76.9 us
    unnamed x1, local copies, waits for them, and re-layouts  2.3 us

profile of v3, /device:TPU:1, one launch (start us, length us, event | category | flops | bytes accessed | tf_op | source)
XLA Modules:
  0.0 80.6 jit_solution(4772286398422323830)
XLA Ops:
  0.0 0.7 fusion
  0.7 0.1 copy.10
  0.8 0.6 pad_convert_fusion.flag_ref
  1.4 76.9 %shard_map.73 = bf16[256,2048]{1,0:T(8,128)(2,1)} custom-call(bf16[256,1024]{1,0:T(8,128)(2,1)} %q_hbm.1, bf16[16,128]{1,0:T(8,128)(2,1)} %pad_convert_fusion.flag_ref, bf16[256,1024]{1,0:T(8,128)(2,1)} %span_k_hbm.1, bf16[256,1024]{1,0:T(8,128)(2,1)} %span_v_hbm.1, bf16[512,1024]{1,0:T(8,128)(2,1)} %k_hbm.1, bf16[512,1024]{1,0:T(8,128)(2,1)} %v_hbm.1, ...), custom_call_target="tpu_custom_call" | custom-call | flops 4294967296 | bytes 16777216 | tf_op jit(solution)/shard_map/pallas_call | solution.py:614
  78.3 2.3 %copy.12 = bf16[256,2048]{1,0:T(8,128)(2,1)} copy(bf16[256,2048]{1,0:T(8,128)(2,1)} %shard_map.73) | data formatting | bytes 2097152
  (1 shorter events, 0.0 us)

commit v4 on v3

--- a/solution.py
+++ b/solution.py
@@ -124,6 +124,7 @@
 BIG = 1e30
 LOG2E = math.log2(math.e)
 LANES = 128
+HOP = 2
 VALUE_ROWS = DH + 16
 
 
@@ -511,7 +512,7 @@
     def _(h):
         q_copy(h).wait()
 
-    @pl.loop(1, heads + 2 * last + 1)
+    @pl.loop(1, heads + last + HOP * last + 1)
     def _(t):
         gather_step(t)
         h = t - last
@@ -522,6 +523,9 @@
             read_flags()
             for copy in own_copies:
                 copy.wait()
+
+        reduce_step(h - HOP * z, 1)
+        reduce_step(h - HOP * (last - z), -1)
 
         @pl.when(busy)
         def _():
@@ -536,16 +540,15 @@
                         for copy in rs_copies(h, s, step):
                             copy.start()
 
-        reduce_step(h - z, 1)
-        reduce_step(h - last + z, -1)
-
         @pl.when(busy)
         def _():
             self_part(h)
 
-        @pl.when((h >= last) & (h < heads + last))
-        def _():
-            finish(h - last)
+        done = h - HOP * last
+
+        @pl.when((done >= 0) & (done < heads))
+        def _():
+            finish(done)
 
     w_local.wait()
     w_remote.wait()

time: 80.8 us -> 77.8 us (0.963)
  Pallas kernels: 76.9 us -> 73.9 us
    pallas_call x1, Pallas kernels: 76.9 us -> 73.9 us  [routed_by_lines(): pl.pallas_call(functools.partial(kernel, stages, heads, blocks), out_shap...]
where the time goes in v4:
time: 77.8 us; the launch traced here: 77.6 us
  Pallas kernels  73.9 us (95%)
  local copies, waits for them, and re-layouts  2.42 us (3%)
  other arithmetic  1.3 us (2%)
    pallas_call x1, Pallas kernels, routed_by_lines(): pl.pallas_call(functools.partial(kernel, stages, heads, blocks), out_shap...  73.9 us
    unnamed x1, local copies, waits for them, and re-layouts  2.3 us

profile of v4, /device:TPU:1, one launch (start us, length us, event | category | flops | bytes accessed | tf_op | source)
XLA Modules:
  0.0 77.6 jit_solution(18160968679268326879)
XLA Ops:
  0.0 0.7 fusion
  0.7 0.1 copy.10
  0.8 0.6 pad_convert_fusion.flag_ref
  1.4 73.9 %shard_map.73 = bf16[256,2048]{1,0:T(8,128)(2,1)} custom-call(bf16[256,1024]{1,0:T(8,128)(2,1)} %q_hbm.1, bf16[16,128]{1,0:T(8,128)(2,1)} %pad_convert_fusion.flag_ref, bf16[256,1024]{1,0:T(8,128)(2,1)} %span_k_hbm.1, bf16[256,1024]{1,0:T(8,128)(2,1)} %span_v_hbm.1, bf16[512,1024]{1,0:T(8,128)(2,1)} %k_hbm.1, bf16[512,1024]{1,0:T(8,128)(2,1)} %v_hbm.1, ...), custom_call_target="tpu_custom_call" | custom-call | flops 4294967296 | bytes 16777216 | tf_op jit(solution)/shard_map/pallas_call | solution.py:617
  75.3 2.3 %copy.12 = bf16[256,2048]{1,0:T(8,128)(2,1)} copy(bf16[256,2048]{1,0:T(8,128)(2,1)} %shard_map.73) | data formatting | bytes 2097152
  (1 shorter events, 0.0 us)
